TPU v7x, 256 devices: a whole 4x4x8 slice. The times are simulated.
256 devices in a mesh: tm: 32 (over y_lo, z, core), gy: 8 (over y_hi, x).
Axes of the slice: x: 4, y: 4 (y_hi: 2, y_lo: 2; y = y_hi * 2 + y_lo), z: 8, core: 2. Of those that a mesh axis runs over, the one named last changes fastest.
Arguments:
- magnetic: bfloat16 [32, 3, 3, 1024, 1024], P('tm', None, None, 'gy'), may hold values from -6 to 6
- velocity: bfloat16 [32, 3, 1, 1024, 1024], P('tm', None, None, 'gy'), may hold values from -6 to 6
- mode_bin: int32 [1024, 1024], P(None, 'gy'), may hold values from 0 to 127, as said below
- omega_edges: int32 [9], replicated, may hold values from 0 to 32, as said below
Outputs:
- power: float32 [32, 1024, 1024], P('tm', None, 'gy')
- spectrum: float32 [8, 128], replicated
Inputs may be any that keep to these rules, and one draw needn't show every extreme that they name: mode_bin = 16 * p + q, where p is a level of min(kz, 1024 - kz) and q a level of min(ky, 1024 - ky); levels never fall as the wavenumber rises, and every value occurs. `omega_edges`: edges rise strictly, the first 0 and the last 32.
All inputs are finite; a program needn't handle non-finite values.
Results may differ from a plain program's by a relative error of at most 0.004.
The roundings to bfloat16 on the way count: a program that leaves them out, or rounds other values in their place, can miss the bound.
Values may be sent and summed in bfloat16 or wider, within the bound.
No kernel may reach another device: no remote copies, remote signals or barrier semaphores. Data moves between devices by JAX's collectives and lax.ppermute only.
A program may use at most 128 MiB of HBM per device.

v0:
```python
import math
import jax
import jax.numpy as jnp
from jax import lax
from jax.sharding import PartitionSpec as P

NBP = 8
NBQ = 16
NB_W = 8
hall_coef = 1.0
highest = lax.Precision.HIGHEST


def extended(cells, sides, width):
    for axis, dim in sides:
        count = lax.axis_size(axis)
        head = lax.slice_in_dim(cells, 0, width, axis=dim)
        tail = lax.slice_in_dim(cells, cells.shape[dim] - width, cells.shape[dim], axis=dim)
        cells = jnp.concatenate(
            [
                lax.ppermute(tail, axis, [(i, (i + 1) % count) for i in range(count)]),
                cells,
                lax.ppermute(head, axis, [((i + 1) % count, i) for i in range(count)]),
            ],
            axis=dim,
        )
    return cells


def window_taper_for(sample_moments, every_time_sample):
    return 0.5 - 0.5 * jnp.cos(
        2.0 * math.pi * (sample_moments.astype(jnp.float32) + 0.5) / every_time_sample
    )


def temporal_coefficients(angular_frequency, sample_moments, every_time_sample):
    phase_angles = jnp.mod(
        angular_frequency[:, None] * sample_moments[None, :], every_time_sample
    ).astype(jnp.float32)
    angles = 2.0 * math.pi * phase_angles / every_time_sample
    taper_weight = window_taper_for(sample_moments, every_time_sample)[None, :]
    return (
        (taper_weight * jnp.cos(angles)).astype(jnp.bfloat16),
        (-taper_weight * jnp.sin(angles)).astype(jnp.bfloat16),
    )


def dft_tables(length):
    series = jnp.arange(length, dtype=jnp.int32)
    phase_angles = jnp.mod(series[:, None] * series[None, :], length).astype(jnp.float32)
    angles = 2.0 * math.pi * phase_angles / length
    return (jnp.cos(angles).astype(jnp.bfloat16), jnp.sin(angles).astype(jnp.bfloat16))


def z_slope(values):
    return (jnp.roll(values, -1, axis=-1) - jnp.roll(values, 1, axis=-1)) * 0.5


def z_turn(re_part, im_part):
    zcos_tab, zsin_tab = dft_tables(re_part.shape[-1])
    turned_re = jnp.dot(re_part, zcos_tab, preferred_element_type=jnp.float32) + jnp.dot(
        im_part, zsin_tab, preferred_element_type=jnp.float32
    )
    turned_im = jnp.dot(im_part, zcos_tab, preferred_element_type=jnp.float32) - jnp.dot(
        re_part, zsin_tab, preferred_element_type=jnp.float32
    )
    return jnp.stack([turned_re, turned_im]).astype(jnp.bfloat16)


def electric_of(magnetic, velocity, slope_magz, slope_magx):
    inner = magnetic[:, :, 1:-1].astype(jnp.float32)
    x_slope = (
        magnetic[:, :, 2:].astype(jnp.float32) - magnetic[:, :, :-2].astype(jnp.float32)
    ) * 0.5
    mag_x, mag_y, mag_z = (inner[:, 0], inner[:, 1], inner[:, 2])
    cur_x = slope_magz - z_slope(mag_y)
    cur_y = z_slope(mag_x) - x_slope[:, 2]
    cur_z = x_slope[:, 1] - slope_magx
    flow = velocity.astype(jnp.float32)
    vel_x, vel_y, vel_z = (flow[:, 0], flow[:, 1], flow[:, 2])
    elec_x = -(vel_y * mag_z - vel_z * mag_y) + hall_coef * (cur_y * mag_z - cur_z * mag_y)
    elec_y = -(vel_z * mag_x - vel_x * mag_z) + hall_coef * (cur_z * mag_x - cur_x * mag_z)
    elec_z = -(vel_x * mag_y - vel_y * mag_x) + hall_coef * (cur_x * mag_y - cur_y * mag_x)
    return jnp.stack([elec_x, elec_y, elec_z], axis=1)


def body(magnetic, velocity, mode_bin, omega_edges):
    face_rows = jnp.stack([magnetic[:, 2, 1:-1], magnetic[:, 0, 1:-1]], axis=1)
    padded = extended(face_rows, (("gy", 3),), 1)
    slopes = (
        padded[:, :, :, 2:].astype(jnp.float32) - padded[:, :, :, :-2].astype(jnp.float32)
    ) * 0.5
    electric = electric_of(magnetic, velocity, slopes[:, 0], slopes[:, 1]).astype(jnp.bfloat16)
    local_t = electric.shape[0]
    z_count = electric.shape[-1]
    every_time_sample = local_t * lax.axis_size("tm")
    half_count = every_time_sample // 2
    owner_rank = lax.axis_index("tm")
    angular_frequency = owner_rank * local_t + jnp.arange(local_t, dtype=jnp.int32) - half_count
    time_segment = lax.all_gather(electric, "tm", axis=0, tiled=True)
    sample_moments = jnp.arange(time_segment.shape[0], dtype=jnp.int32)
    coefficient_real, coefficient_imaginary = temporal_coefficients(
        angular_frequency, sample_moments, every_time_sample
    )
    re_part = jnp.einsum(
        "wt,tcxyz->wcxyz", coefficient_real, time_segment, preferred_element_type=jnp.float32
    )
    im_part = jnp.einsum(
        "wt,tcxyz->wcxyz", coefficient_imaginary, time_segment, preferred_element_type=jnp.float32
    )
    moved = lax.all_to_all(
        z_turn(re_part.astype(jnp.bfloat16), im_part.astype(jnp.bfloat16)),
        "gy",
        split_axis=5,
        concat_axis=4,
        tiled=True,
    )
    y_count = moved.shape[4]
    ycos_tab, ysin_tab = dft_tables(y_count)
    wave_re = jnp.einsum(
        "wcxyk,yq->wcxqk", moved[0], ycos_tab, preferred_element_type=jnp.float32
    ) + jnp.einsum("wcxyk,yq->wcxqk", moved[1], ysin_tab, preferred_element_type=jnp.float32)
    wave_im = jnp.einsum(
        "wcxyk,yq->wcxqk", moved[1], ycos_tab, preferred_element_type=jnp.float32
    ) - jnp.einsum("wcxyk,yq->wcxqk", moved[0], ysin_tab, preferred_element_type=jnp.float32)
    power_map = jnp.sum(wave_re * wave_re + wave_im * wave_im, axis=(1, 2)) / (
        every_time_sample * y_count * z_count
    )
    kz_local = power_map.shape[2]
    block_rows = min(64, y_count)
    bin_total = NBP * NBQ
    bin_range = jnp.arange(bin_total, dtype=jnp.int32)

    def add_block(step_num, summed):
        row_block = lax.dynamic_slice_in_dim(
            power_map, step_num * block_rows, block_rows, 1
        ).reshape(local_t, block_rows * kz_local)
        bin_ids = lax.dynamic_slice_in_dim(mode_bin, step_num * block_rows, block_rows, 0).reshape(
            block_rows * kz_local
        )
        onehot = (bin_ids[:, None] == bin_range[None, :]).astype(jnp.float32)
        return summed + jnp.dot(row_block, onehot, precision=highest)

    by_mode = lax.fori_loop(
        0, y_count // block_rows, add_block, jnp.zeros((local_t, bin_total), jnp.float32)
    )
    omega = owner_rank * local_t + jnp.arange(local_t, dtype=jnp.int32)
    member = (
        (omega[None, :] >= omega_edges[:-1, None]) & (omega[None, :] < omega_edges[1:, None])
    ).astype(jnp.float32)
    partial_value = jnp.dot(member, by_mode, precision=highest)
    binned = lax.psum(partial_value, ("tm", "gy"))
    spectrum = jnp.log(
        binned * (NB_W * bin_total) / (every_time_sample * y_count * z_count) + 1e-06
    )
    return (power_map, spectrum)


def solution(mesh):
    return jax.shard_map(
        body,
        mesh=mesh,
        in_specs=(
            P("tm", None, None, "gy", None),
            P("tm", None, None, "gy", None),
            P(None, "gy"),
            P(),
        ),
        out_specs=(P("tm", None, "gy"), P()),
        check_vma=False,
    )
```

profile of v0, /device:TPU:1, one launch (start us, length us, event | category | flops | bytes accessed | tf_op | source)
XLA Modules:
  0.0 512.5 jit_solution(18000967554781323091)
XLA Ops:
  8.5 6.0 %collective-permute-start = (bf16[1,2,1,1,1024]{4,3,2,1,0:T(2,128)(2,1)S(1)}, bf16[1,2,1,1,1024]{4,3,2,1,0:T(2,128)(2,1)S(1)}, u32[]{:S(2)}, u32[]{:S(2)}) collective-permute-start(bf16[1,2,1,1,1024]{4,3,2,1,0:T(2,128)(2,1)S(1)} %get-tuple-element.139), channel_id=1, source_target_pairs={{1,0},{2,1},{3,2},{4,3},{5,4},{6,5},{7,6},{0,7},{9,8},{10,9},{11,1... | collective-permute-start | bytes 12296 | tf_op jit(solution)/shard_map/ppermute | solution.py:23
  16.7 3.9 collective-permute-done.1
  23.7 142.3 %all-gather.2.cloned.1.call-done = bf16[32,3,1,128,1024]{4,3,2,1,0:T(8,128)(2,1)} async-done(((bf16[1,3,1,128,1024]{4,3,2,1,0:T(8,128)(2,1)}), bf16[32,3,1,128,1024]{4,3,2,1,0:T(8,128)(2,1)}) %all-gather.2.cloned.1.call-update) | async-done | bytes 25165840 | tf_op jit(solution)/shard_map/all_gather | solution.py:100
  166.0 24.4 %fusion.5 = bf16[1,3,128,1024]{3,0,2,1:T(2,128)(2,1)S(1)} fusion(bf16[32,3,128,1024]{3,2,1,0:T(8,128)(2,1)} %bitcast.97, s32[]{:T(128)S(6)} %sub.139), kind=kOutput, calls=%fused_computation.8 | convolution fusion | flops 25166528 | bytes 25952260 | tf_op jit(solution)/shard_map/wt,tcxyz->wcxyz/dot_general | solution.py:108
  190.5 24.9 %fusion.7 = bf16[1,3,128,1024]{3,0,2,1:T(2,128)(2,1)S(1)} fusion(bf16[32,3,128,1024]{3,2,1,0:T(8,128)(2,1)} %bitcast.98, s32[]{:T(128)S(6)} %sub.139), kind=kOutput, calls=%fused_computation.10 | convolution fusion | flops 25166496 | bytes 25952260 | tf_op jit(solution)/shard_map/wt,tcxyz->wcxyz/dot_general | solution.py:105
  215.4 16.1 %fusion.21 = f32[3,128,1024]{2,1,0:T(8,128)S(1)} fusion(bf16[1,3,128,1024]{3,0,2,1:T(2,128)(2,1)S(1)} %fusion.7), kind=kOutput, calls=%fused_computation.27 | convolution fusion | flops 821035008 | bytes 2359296 | tf_op jit(solution)/shard_map/dot_general | solution.py:64
  231.5 16.1 %fusion.23 = f32[3,128,1024]{2,1,0:T(8,128)S(1)} fusion(bf16[1,3,128,1024]{3,0,2,1:T(2,128)(2,1)S(1)} %fusion.5), kind=kOutput, calls=%fused_computation.28 | convolution fusion | flops 821035008 | bytes 2359296 | tf_op jit(solution)/shard_map/dot_general | solution.py:61
  247.6 16.5 %fusion.42 = bf16[1,1,3,1,128,1024]{5,4,2,3,1,0:T(8,128)(2,1)S(1)} fusion(f32[3,128,1024]{2,1,0:T(8,128)S(1)} %fusion.21, bf16[1,3,128,1024]{3,0,2,1:T(2,128)(2,1)S(1)} %fusion.5), kind=kOutput, calls=%fused_computation.41 | convolution fusion | flops 821821440 | bytes 3145728 | tf_op jit(solution)/shard_map/dot_general | solution.py:64
  264.1 16.3 %fusion.39 = bf16[1,1,3,1,128,1024]{5,4,2,3,1,0:T(8,128)(2,1)S(1)} fusion(f32[3,128,1024]{2,1,0:T(8,128)S(1)} %fusion.23, bf16[1,3,128,1024]{3,0,2,1:T(2,128)(2,1)S(1)} %fusion.7), kind=kOutput, calls=%fused_computation.40 | convolution fusion | flops 821821440 | bytes 3145728 | tf_op jit(solution)/shard_map/dot_general | solution.py:61
  280.6 3.0 copy.44
  283.6 6.7 %all-to-all-start = ((bf16[2,1,3,1,128,1024]{4,0,3,2,1,5:T(2,128)(2,1)}), bf16[2,1,3,1,128,1024]{4,0,3,2,1,5:T(2,128)(2,1)S(1)}, u32[]{:S(2)}, u32[]{:S(2)}) async-start(bf16[2,1,3,1,128,1024]{4,0,3,2,1,5:T(2,128)(2,1)} %copy.44), calls=%async_computation | async-start | bytes 3145728 | tf_op jit(solution)/shard_map/all_to_all | solution.py:111
  290.4 22.9 %all-to-all-done = bf16[2,1,3,1,128,1024]{4,0,3,2,1,5:T(2,128)(2,1)S(1)} async-done(((bf16[2,1,3,1,128,1024]{4,0,3,2,1,5:T(2,128)(2,1)}), bf16[2,1,3,1,128,1024]{4,0,3,2,1,5:T(2,128)(2,1)S(1)}, u32[]{:S(2)}, u32[]{:S(2)}) %all-to-all-start) | async-done | bytes 1572896 | tf_op jit(solution)/shard_map/all_to_all | solution.py:111
  313.3 2.4 copy.45
  315.8 17.9 %fusion.29 = f32[1024,3,128]{2,0,1:T(8,128)S(1)} fusion(bf16[3,1024,128]{2,1,0:T(8,128)(2,1)S(1)} %bitcast.104), kind=kOutput, calls=%fused_computation.31 | convolution fusion | flops 821035008 | bytes 2359296 | tf_op jit(solution)/shard_map/wcxyk,yq->wcxqk/dot_general | solution.py:123
  333.7 18.0 %fusion.19 = f32[1024,3,128]{2,0,1:T(8,128)S(1)} fusion(bf16[3,1024,128]{2,1,0:T(8,128)(2,1)S(1)} %bitcast.105), kind=kOutput, calls=%fused_computation.26 | convolution fusion | flops 821035008 | bytes 2359296 | tf_op jit(solution)/shard_map/wcxyk,yq->wcxqk/dot_general | solution.py:122
  351.6 18.0 %fusion.17 = f32[1024,3,128]{2,0,1:T(8,128)S(1)} fusion(bf16[3,1024,128]{2,1,0:T(8,128)(2,1)S(1)} %bitcast.102), kind=kOutput, calls=%fused_computation.25 | convolution fusion | flops 821035008 | bytes 2359296 | tf_op jit(solution)/shard_map/wcxyk,yq->wcxqk/dot_general | solution.py:125
  369.6 18.0 %add_reduce_fusion = f32[1024,128]{1,0:T(8,128)S(1)} fusion(f32[1024,3,128]{2,0,1:T(8,128)S(1)} %fusion.29, f32[1024,3,128]{2,0,1:T(8,128)S(1)} %fusion.17, f32[1024,3,128]{2,0,1:T(8,128)S(1)} %fusion.19, bf16[3,1024,128]{2,1,0:T(8,128)(2,1)S(1)} %bitcast.103), kind=kOutput, calls=%fused_computation.36 | convolution fusion | flops 823263232 | bytes 6029312 | tf_op jit(solution)/shard_map/wcxyk,yq->wcxqk/dot_general | solution.py:120
  387.7 41.5 %while.14 = (s32[]{:T(128)}, f32[1,128]{1,0:T(1,128)S(1)}, f32[1,1024,128]{2,1,0:T(8,128)S(1)}, s32[1024,128]{1,0:T(8,128)}, s32[]{:T(128)}, /*index=5*/s32[]{:T(128)}, s32[]{:T(128)}, s32[]{:T(128)}) while((s32[]{:T(128)}, f32[1,128]{1,0:T(1,128)S(1)}, f32[1,1024,128]{2,1,0:T(8,128)S(1)}, s32[1024,128]{1,0:T(8,128)}, s32[]{:T(128)}, ...), condition=%wide.region_2.3_spmd.clone, body=%wide.region_1.2_spmd.clone.sunk | while | flops 13631751 | bytes 197789 | solution.py:144
  388.5 1.8 fusion.113
  393.7 1.8 fusion.113
  396.3 1.8 fusion.113
  398.9 1.8 fusion.113
  401.5 1.8 fusion.113
  429.3 75.6 %psum.7 = f32[8,128]{1,0:T(8,128)S(1)} all-reduce(f32[8,128]{1,0:T(8,128)S(1)} %broadcast_multiply_fusion), channel_id=1, replica_groups=mesh['tm'=32,'gy'=8] {'tm','gy'}, use_global_device_ids=true, to_apply=%region_3.4 | all-reduce | flops 1024 | bytes 8192 | tf_op jit(solution)/shard_map/psum | solution.py:152
  (77 shorter events, 39.6 us)
Async XLA Ops:
  7.2 8.7 %copy-start = (bf16[1,3,3,128,1024]{4,3,2,1,0:T(8,128)(2,1)S(1)}, bf16[1,3,3,128,1024]{4,3,2,1,0:T(8,128)(2,1)}, u32[]{:S(2)}) copy-start(bf16[1,3,3,128,1024]{4,3,2,1,0:T(8,128)(2,1)} %param.6) | copy-start | bytes 7077892
  7.2 158.9 %all-gather.2.cloned.1.call-start = ((), (), s32[]{:S(2)}) async-start(), calls=%async_computation.1 | async-start | bytes 25952256 | tf_op jit(solution)/shard_map/all_gather | solution.py:100
  8.5 8.2 %collective-permute-start = (bf16[1,2,1,1,1024]{4,3,2,1,0:T(2,128)(2,1)S(1)}, bf16[1,2,1,1,1024]{4,3,2,1,0:T(2,128)(2,1)S(1)}, u32[]{:S(2)}, u32[]{:S(2)}) collective-permute-start(bf16[1,2,1,1,1024]{4,3,2,1,0:T(2,128)(2,1)S(1)} %get-tuple-element.139), channel_id=1, source_target_pairs={{1,0},{2,1},{3,2},{4,3},{5,4},{6,5},{7,6},{0,7},{9,8},{10,9},{11,1... | collective-permute-start | bytes 12296 | tf_op jit(solution)/shard_map/ppermute | solution.py:23
  14.5 2.0 copy-start.2
  14.5 6.1 %collective-permute-start.1 = (bf16[1,2,1,1,1024]{4,3,2,1,0:T(2,128)(2,1)S(1)}, bf16[1,2,1,1,1024]{4,3,2,1,0:T(2,128)(2,1)S(1)}, u32[]{:S(2)}, u32[]{:S(2)}) collective-permute-start(bf16[1,2,1,1,1024]{4,3,2,1,0:T(2,128)(2,1)S(1)} %get-tuple-element.140), channel_id=1, source_target_pairs={{0,1},{1,2},{2,3},{3,4},{4,5},{5,6},{6,7},{7,0},{8,9},{9,10},{10,1... | collective-permute-start | bytes 12296 | tf_op jit(solution)/shard_map/ppermute | solution.py:21
  280.4 9.9 %copy-start.3 = (s32[9]{0:T(128)S(1)}, s32[9]{0:T(128)}, u32[]{:S(2)}) copy-start(s32[9]{0:T(128)} %param.9) | copy-start | bytes 112
  283.6 29.7 %all-to-all-start = ((bf16[2,1,3,1,128,1024]{4,0,3,2,1,5:T(2,128)(2,1)}), bf16[2,1,3,1,128,1024]{4,0,3,2,1,5:T(2,128)(2,1)S(1)}, u32[]{:S(2)}, u32[]{:S(2)}) async-start(bf16[2,1,3,1,128,1024]{4,0,3,2,1,5:T(2,128)(2,1)} %copy.44), calls=%async_computation | async-start | bytes 3145728 | tf_op jit(solution)/shard_map/all_to_all | solution.py:111
  429.2 76.3 %copy-start.1 = (f32[1,1024,128]{2,1,0:T(8,128)}, f32[1,1024,128]{2,1,0:T(8,128)S(1)}, u32[]{:S(2)}) copy-start(f32[1,1024,128]{2,1,0:T(8,128)S(1)} %get-tuple-element.195) | copy-start | bytes 1572868
Sparse Core Ops, SparseCore 0:
  23.8 142.1 all-gather.1
where the time goes:
time: 518 us; the launch traced here: 513 us
  matrix products  215 us (42%)
  waiting for transfers between devices  169 us (33%)
  blocking collectives  75.6 us (15%)
  local copies, waits for them, and re-layouts  19.7 us (4%)
  between operations  14.5 us (3%)
  starting transfers between devices  12.7 us (2%)
  other arithmetic  5.55 us (1%)
    all_gather x1, waiting for transfers between devices, body(): time_segment = lax.all_gather(electric, 'tm', axis=0, tiled=True)  142 us
    psum x1, blocking collectives, body(): binned = lax.psum(partial_value, ('tm', 'gy'))  75.6 us
    dot_general x16, matrix products, add_block(): return summed + jnp.dot(row_block, onehot, precision=highest)  28.7 us
    dot_general x1, matrix products, body(): jnp.einsum('wt,tcxyz->wcxyz', coefficient_real, time_segment, preferred_e...  24.9 us
    dot_general x1, matrix products, body(): jnp.einsum('wt,tcxyz->wcxyz', coefficient_imaginary, time_segment, prefer...  24.4 us
    all_to_all x1, waiting for transfers between devices, body(): lax.all_to_all(z_turn(re_part.astype(jnp.bfloat16), im_part.astype(jnp.bf...  22.9 us
    dot_general x1, matrix products, body(): jnp.einsum('wcxyk,yq->wcxqk', moved[0], ycos_tab, preferred_element_type=...  18 us
    dot_general x1, matrix products, body(): jnp.einsum('wcxyk,yq->wcxqk', moved[1], ysin_tab, preferred_element_type=...  18 us
  transfers between devices with their start and end apart: 4, of which 3 were waited for; matrix products, arithmetic and copies ran while one was open for 0% of the time, Pallas kernels for 0%

commit v1 on v0

--- a/solution.py
+++ b/solution.py
@@ -149,7 +149,7 @@
         (omega[None, :] >= omega_edges[:-1, None]) & (omega[None, :] < omega_edges[1:, None])
     ).astype(jnp.float32)
     partial_value = jnp.dot(member, by_mode, precision=highest)
-    binned = lax.psum(partial_value, ("tm", "gy"))
+    binned = lax.psum(lax.psum(partial_value, "gy"), "tm")
     spectrum = jnp.log(
         binned * (NB_W * bin_total) / (every_time_sample * y_count * z_count) + 1e-06
     )

time: 518 us -> 517 us (level)
    psum x1 -> x2, blocking collectives: 75.6 us -> 75.1 us  [body(): binned = lax.psum(lax.psum(partial_value, 'gy'), 'tm')]
where the time goes in v1:
time: 517 us; the launch traced here: 512 us
  matrix products  215 us (42%)
  waiting for transfers between devices  169 us (33%)
  blocking collectives  75.1 us (15%)
  local copies, waits for them, and re-layouts  19.6 us (4%)
  between operations  14.5 us (3%)
  starting transfers between devices  12.7 us (2%)
  other arithmetic  5.53 us (1%)
    all_gather x1, waiting for transfers between devices, body(): time_segment = lax.all_gather(electric, 'tm', axis=0, tiled=True)  142 us
    psum x2, blocking collectives, body(): binned = lax.psum(lax.psum(partial_value, 'gy'), 'tm')  75.1 us
    dot_general x16, matrix products, add_block(): return summed + jnp.dot(row_block, onehot, precision=highest)  28.7 us
    dot_general x1, matrix products, body(): jnp.einsum('wt,tcxyz->wcxyz', coefficient_real, time_segment, preferred_e...  24.9 us
    dot_general x1, matrix products, body(): jnp.einsum('wt,tcxyz->wcxyz', coefficient_imaginary, time_segment, prefer...  24.4 us
    all_to_all x1, waiting for transfers between devices, body(): lax.all_to_all(z_turn(re_part.astype(jnp.bfloat16), im_part.astype(jnp.bf...  22.9 us
    dot_general x1, matrix products, body(): jnp.einsum('wcxyk,yq->wcxqk', moved[0], ycos_tab, preferred_element_type=...  18 us
    dot_general x1, matrix products, body(): jnp.einsum('wcxyk,yq->wcxqk', moved[1], ysin_tab, preferred_element_type=...  18 us
  transfers between devices with their start and end apart: 4, of which 3 were waited for; matrix products, arithmetic and copies ran while one was open for 0% of the time, Pallas kernels for 0%

profile of v1, /device:TPU:1, one launch (start us, length us, event | category | flops | bytes accessed | tf_op | source)
XLA Modules:
  0.0 511.9 jit_solution(6100909402852429790)
XLA Ops:
  8.5 6.0 %collective-permute-start = (bf16[1,2,1,1,1024]{4,3,2,1,0:T(2,128)(2,1)S(1)}, bf16[1,2,1,1,1024]{4,3,2,1,0:T(2,128)(2,1)S(1)}, u32[]{:S(2)}, u32[]{:S(2)}) collective-permute-start(bf16[1,2,1,1,1024]{4,3,2,1,0:T(2,128)(2,1)S(1)} %get-tuple-element.139), channel_id=1, source_target_pairs={{1,0},{2,1},{3,2},{4,3},{5,4},{6,5},{7,6},{0,7},{9,8},{10,9},{11,1... | collective-permute-start | bytes 12296 | tf_op jit(solution)/shard_map/ppermute | solution.py:23
  16.7 3.9 collective-permute-done.1
  23.7 142.3 %all-gather.2.cloned.1.call-done = bf16[32,3,1,128,1024]{4,3,2,1,0:T(8,128)(2,1)} async-done(((bf16[1,3,1,128,1024]{4,3,2,1,0:T(8,128)(2,1)}), bf16[32,3,1,128,1024]{4,3,2,1,0:T(8,128)(2,1)}) %all-gather.2.cloned.1.call-update) | async-done | bytes 25165840 | tf_op jit(solution)/shard_map/all_gather | solution.py:100
  166.0 24.4 %fusion.5 = bf16[1,3,128,1024]{3,0,2,1:T(2,128)(2,1)S(1)} fusion(bf16[32,3,128,1024]{3,2,1,0:T(8,128)(2,1)} %bitcast.97, s32[]{:T(128)S(6)} %sub.139), kind=kOutput, calls=%fused_computation.8 | convolution fusion | flops 25166528 | bytes 25952260 | tf_op jit(solution)/shard_map/wt,tcxyz->wcxyz/dot_general | solution.py:108
  190.5 24.9 %fusion.7 = bf16[1,3,128,1024]{3,0,2,1:T(2,128)(2,1)S(1)} fusion(bf16[32,3,128,1024]{3,2,1,0:T(8,128)(2,1)} %bitcast.98, s32[]{:T(128)S(6)} %sub.139), kind=kOutput, calls=%fused_computation.10 | convolution fusion | flops 25166496 | bytes 25952260 | tf_op jit(solution)/shard_map/wt,tcxyz->wcxyz/dot_general | solution.py:105
  215.4 16.1 %fusion.21 = f32[3,128,1024]{2,1,0:T(8,128)S(1)} fusion(bf16[1,3,128,1024]{3,0,2,1:T(2,128)(2,1)S(1)} %fusion.7), kind=kOutput, calls=%fused_computation.27 | convolution fusion | flops 821035008 | bytes 2359296 | tf_op jit(solution)/shard_map/dot_general | solution.py:64
  231.5 16.1 %fusion.23 = f32[3,128,1024]{2,1,0:T(8,128)S(1)} fusion(bf16[1,3,128,1024]{3,0,2,1:T(2,128)(2,1)S(1)} %fusion.5), kind=kOutput, calls=%fused_computation.28 | convolution fusion | flops 821035008 | bytes 2359296 | tf_op jit(solution)/shard_map/dot_general | solution.py:61
  247.6 16.5 %fusion.42 = bf16[1,1,3,1,128,1024]{5,4,2,3,1,0:T(8,128)(2,1)S(1)} fusion(f32[3,128,1024]{2,1,0:T(8,128)S(1)} %fusion.21, bf16[1,3,128,1024]{3,0,2,1:T(2,128)(2,1)S(1)} %fusion.5), kind=kOutput, calls=%fused_computation.41 | convolution fusion | flops 821821440 | bytes 3145728 | tf_op jit(solution)/shard_map/dot_general | solution.py:64
  264.1 16.3 %fusion.39 = bf16[1,1,3,1,128,1024]{5,4,2,3,1,0:T(8,128)(2,1)S(1)} fusion(f32[3,128,1024]{2,1,0:T(8,128)S(1)} %fusion.23, bf16[1,3,128,1024]{3,0,2,1:T(2,128)(2,1)S(1)} %fusion.7), kind=kOutput, calls=%fused_computation.40 | convolution fusion | flops 821821440 | bytes 3145728 | tf_op jit(solution)/shard_map/dot_general | solution.py:61
  280.6 3.0 copy.44
  283.6 6.7 %all-to-all-start = ((bf16[2,1,3,1,128,1024]{4,0,3,2,1,5:T(2,128)(2,1)}), bf16[2,1,3,1,128,1024]{4,0,3,2,1,5:T(2,128)(2,1)S(1)}, u32[]{:S(2)}, u32[]{:S(2)}) async-start(bf16[2,1,3,1,128,1024]{4,0,3,2,1,5:T(2,128)(2,1)} %copy.44), calls=%async_computation | async-start | bytes 3145728 | tf_op jit(solution)/shard_map/all_to_all | solution.py:111
  290.3 22.9 %all-to-all-done = bf16[2,1,3,1,128,1024]{4,0,3,2,1,5:T(2,128)(2,1)S(1)} async-done(((bf16[2,1,3,1,128,1024]{4,0,3,2,1,5:T(2,128)(2,1)}), bf16[2,1,3,1,128,1024]{4,0,3,2,1,5:T(2,128)(2,1)S(1)}, u32[]{:S(2)}, u32[]{:S(2)}) %all-to-all-start) | async-done | bytes 1572896 | tf_op jit(solution)/shard_map/all_to_all | solution.py:111
  313.2 2.4 copy.45
  315.7 17.9 %fusion.29 = f32[1024,3,128]{2,0,1:T(8,128)S(1)} fusion(bf16[3,1024,128]{2,1,0:T(8,128)(2,1)S(1)} %bitcast.104), kind=kOutput, calls=%fused_computation.31 | convolution fusion | flops 821035008 | bytes 2359296 | tf_op jit(solution)/shard_map/wcxyk,yq->wcxqk/dot_general | solution.py:123
  333.6 18.0 %fusion.19 = f32[1024,3,128]{2,0,1:T(8,128)S(1)} fusion(bf16[3,1024,128]{2,1,0:T(8,128)(2,1)S(1)} %bitcast.105), kind=kOutput, calls=%fused_computation.26 | convolution fusion | flops 821035008 | bytes 2359296 | tf_op jit(solution)/shard_map/wcxyk,yq->wcxqk/dot_general | solution.py:122
  351.6 18.0 %fusion.17 = f32[1024,3,128]{2,0,1:T(8,128)S(1)} fusion(bf16[3,1024,128]{2,1,0:T(8,128)(2,1)S(1)} %bitcast.102), kind=kOutput, calls=%fused_computation.25 | convolution fusion | flops 821035008 | bytes 2359296 | tf_op jit(solution)/shard_map/wcxyk,yq->wcxqk/dot_general | solution.py:125
  369.5 18.0 %add_reduce_fusion = f32[1024,128]{1,0:T(8,128)S(1)} fusion(f32[1024,3,128]{2,0,1:T(8,128)S(1)} %fusion.29, f32[1024,3,128]{2,0,1:T(8,128)S(1)} %fusion.17, f32[1024,3,128]{2,0,1:T(8,128)S(1)} %fusion.19, bf16[3,1024,128]{2,1,0:T(8,128)(2,1)S(1)} %bitcast.103), kind=kOutput, calls=%fused_computation.36 | convolution fusion | flops 823263232 | bytes 6029312 | tf_op jit(solution)/shard_map/wcxyk,yq->wcxqk/dot_general | solution.py:120
  387.6 41.5 %while.14 = (s32[]{:T(128)}, f32[1,128]{1,0:T(1,128)S(1)}, f32[1,1024,128]{2,1,0:T(8,128)S(1)}, s32[1024,128]{1,0:T(8,128)}, s32[]{:T(128)}, /*index=5*/s32[]{:T(128)}, s32[]{:T(128)}, s32[]{:T(128)}) while((s32[]{:T(128)}, f32[1,128]{1,0:T(1,128)S(1)}, f32[1,1024,128]{2,1,0:T(8,128)S(1)}, s32[1024,128]{1,0:T(8,128)}, s32[]{:T(128)}, ...), condition=%wide.region_2.3_spmd.clone, body=%wide.region_1.2_spmd.clone.sunk | while | flops 13631751 | bytes 197789 | solution.py:144
  391.0 1.8 fusion.113
  393.6 1.8 fusion.113
  398.8 1.8 fusion.113
  401.4 1.8 fusion.113
  429.2 17.7 %psum.14 = f32[8,128]{1,0:T(8,128)S(1)} all-reduce(f32[8,128]{1,0:T(8,128)S(1)} %broadcast_multiply_fusion), channel_id=1, replica_groups=mesh['tm'=32,'gy'=8] {'gy'}, use_global_device_ids=true, to_apply=%region_3.4 | all-reduce | flops 1024 | bytes 8192 | tf_op jit(solution)/shard_map/psum | solution.py:152
  446.9 57.3 %psum.15 = f32[8,128]{1,0:T(8,128)S(1)} all-reduce(f32[8,128]{1,0:T(8,128)S(1)} %psum.14), channel_id=1, replica_groups=mesh['tm'=32,'gy'=8] {'tm'}, use_global_device_ids=true, to_apply=%region_4.5 | all-reduce | flops 1024 | bytes 8192 | tf_op jit(solution)/shard_map/psum | solution.py:152
  (78 shorter events, 41.4 us)
Async XLA Ops:
  7.2 8.7 %copy-start = (bf16[1,3,3,128,1024]{4,3,2,1,0:T(8,128)(2,1)S(1)}, bf16[1,3,3,128,1024]{4,3,2,1,0:T(8,128)(2,1)}, u32[]{:S(2)}) copy-start(bf16[1,3,3,128,1024]{4,3,2,1,0:T(8,128)(2,1)} %param.6) | copy-start | bytes 7077892
  7.2 158.9 %all-gather.2.cloned.1.call-start = ((), (), s32[]{:S(2)}) async-start(), calls=%async_computation.1 | async-start | bytes 25952256 | tf_op jit(solution)/shard_map/all_gather | solution.py:100
  8.5 8.2 %collective-permute-start = (bf16[1,2,1,1,1024]{4,3,2,1,0:T(2,128)(2,1)S(1)}, bf16[1,2,1,1,1024]{4,3,2,1,0:T(2,128)(2,1)S(1)}, u32[]{:S(2)}, u32[]{:S(2)}) collective-permute-start(bf16[1,2,1,1,1024]{4,3,2,1,0:T(2,128)(2,1)S(1)} %get-tuple-element.139), channel_id=1, source_target_pairs={{1,0},{2,1},{3,2},{4,3},{5,4},{6,5},{7,6},{0,7},{9,8},{10,9},{11,1... | collective-permute-start | bytes 12296 | tf_op jit(solution)/shard_map/ppermute | solution.py:23
  14.5 2.0 copy-start.2
  14.5 6.1 %collective-permute-start.1 = (bf16[1,2,1,1,1024]{4,3,2,1,0:T(2,128)(2,1)S(1)}, bf16[1,2,1,1,1024]{4,3,2,1,0:T(2,128)(2,1)S(1)}, u32[]{:S(2)}, u32[]{:S(2)}) collective-permute-start(bf16[1,2,1,1,1024]{4,3,2,1,0:T(2,128)(2,1)S(1)} %get-tuple-element.140), channel_id=1, source_target_pairs={{0,1},{1,2},{2,3},{3,4},{4,5},{5,6},{6,7},{7,0},{8,9},{9,10},{10,1... | collective-permute-start | bytes 12296 | tf_op jit(solution)/shard_map/ppermute | solution.py:21
  280.4 9.8 %copy-start.3 = (s32[9]{0:T(128)S(1)}, s32[9]{0:T(128)}, u32[]{:S(2)}) copy-start(s32[9]{0:T(128)} %param.9) | copy-start | bytes 112
  283.6 29.6 %all-to-all-start = ((bf16[2,1,3,1,128,1024]{4,0,3,2,1,5:T(2,128)(2,1)}), bf16[2,1,3,1,128,1024]{4,0,3,2,1,5:T(2,128)(2,1)S(1)}, u32[]{:S(2)}, u32[]{:S(2)}) async-start(bf16[2,1,3,1,128,1024]{4,0,3,2,1,5:T(2,128)(2,1)} %copy.44), calls=%async_computation | async-start | bytes 3145728 | tf_op jit(solution)/shard_map/all_to_all | solution.py:111
  429.1 75.7 %copy-start.1 = (f32[1,1024,128]{2,1,0:T(8,128)}, f32[1,1024,128]{2,1,0:T(8,128)S(1)}, u32[]{:S(2)}) copy-start(f32[1,1024,128]{2,1,0:T(8,128)S(1)} %get-tuple-element.195) | copy-start | bytes 1572868
Sparse Core Ops, SparseCore 0:
  23.8 142.1 all-gather.1
